TPU v7x, 512 devices: a whole 4x8x8 slice. The times are simulated.
512 devices in a mesh: row: 32 (over y_hi, z), col: 16 (over x, y_lo, core).
Axes of the slice: x: 4, y: 8 (y_hi: 4, y_lo: 2; y = y_hi * 2 + y_lo), z: 8, core: 2. Of those that a mesh axis runs over, the one named last changes fastest.
Arguments:
- anc_inverse: bfloat16 [1, 32, 256, 2, 16, 256], P(None, 'row', None, None, 'col'), may hold values from -6 to 6
- factor_one: bfloat16 [1, 32, 256, 2, 16, 256], P(None, 'row', None, None, 'col'), may hold values from -0.0625 to 0.0625
- factor_two: bfloat16 [1, 32, 256, 1, 16, 256], P(None, 'row', None, None, 'col'), may hold values from -0.0625 to 0.0625
- parent_block: bfloat16 [1, 16, 256, 256], P(None, 'col'), may hold values from -0.375 to 0.375
- diag_one: float32 [2, 16, 256, 256], P(None, 'col'), may hold values from -6 to 6
- diag_two: float32 [1, 16, 256, 256], P(None, 'col'), may hold values from -6 to 6
- pattern_one: int32 [1, 32, 2, 16], P(None, 'row', None, 'col'), may hold values from 0 to 1
- pattern_two: int32 [1, 32, 1, 16], P(None, 'row', None, 'col'), may hold values from 0 to 1, as said below
- parent: int32 [1, 16], P(None, 'col'), may hold values from 0 to 31, as said below
Outputs:
- inv_one: bfloat16 [1, 32, 256, 2, 16, 256], P(None, 'row', None, None, 'col')
- diag_inv_one: float32 [2, 16, 256, 256], P(None, 'col')
- inv_two: bfloat16 [1, 32, 256, 1, 16, 256], P(None, 'row', None, None, 'col')
- parent_inv: bfloat16 [1, 16, 256, 256], P(None, 'col')
- diag_inv_two: float32 [1, 16, 256, 256], P(None, 'col')
Inputs may be any that keep to these rules, and one draw needn't show every extreme that they name: pattern_two[J, K] is zero wherever pattern_one[J, P(K)] is zero. parent[k, c] is a level-one supernode whose index leaves remainder c when divided by 16.
All inputs are finite; a program needn't handle non-finite values.
Results may differ from a plain program's by a relative error of at most 0.007.
Values may be sent and summed in bfloat16 or wider, within the bound.
A program may use at most 64 MiB of HBM per device.

v0:
```python
import jax
import jax.numpy as jnp
from jax import lax
from jax.sharding import PartitionSpec as P


def rows_step(whole_anc, anc_rows, block):

    def add_rows(total, piece, start):
        count = piece.shape[1]
        left = whole_anc.reshape(anc_rows * block, anc_rows * count * block)
        right = piece.reshape(anc_rows * count * block, piece.shape[3] * block)
        return jnp.dot(left, right, preferred_element_type=jnp.float32)

    return add_rows


def body(
    anc_inverse,
    factor_one,
    factor_two,
    parent_block,
    diag_one,
    diag_two,
    pattern_one,
    pattern_two,
    parent,
):
    anc_rows = anc_inverse.shape[0]
    block = anc_inverse.shape[2]
    first_count = factor_one.shape[3]
    second_count = factor_two.shape[3]
    grid_rows = lax.axis_size("row")
    grid_cols = lax.axis_size("col")
    first_factor = factor_one * pattern_one.astype(jnp.bfloat16)[:, :, None, :, :, None]
    second_factor = factor_two * pattern_two.astype(jnp.bfloat16)[:, :, None, :, :, None]
    first_empty = jnp.zeros((anc_rows * block, first_count * block), jnp.float32)
    second_empty = jnp.zeros((anc_rows * block, second_count * block), jnp.float32)
    whole_anc = lax.all_gather(anc_inverse, "col", axis=4, tiled=True).reshape(
        anc_rows * block, anc_rows, grid_rows, block
    )
    add_rows = rows_step(whole_anc, anc_rows, block)
    first_total = add_rows(
        first_empty, lax.all_gather(first_factor, "row", axis=1, tiled=True), jnp.int32(0)
    )
    first_shape = (anc_rows, block, first_count, block)
    second_shape = (anc_rows, block, second_count, block)
    first_keep = pattern_one.astype(jnp.float32)
    second_keep = pattern_two.astype(jnp.float32)
    first_inv = (-first_total.reshape(first_shape) * first_keep).astype(jnp.bfloat16)
    first_cols = first_factor.reshape(first_shape)
    second_cols = second_factor.reshape(second_shape)
    diag_part = jnp.einsum(
        "ixky,ixkz->kyz", first_cols, first_inv, preferred_element_type=jnp.float32
    )
    local_parent = parent.reshape(second_count) // grid_cols
    parent_cols = jnp.take(first_inv, local_parent, axis=2)
    cross_part = jnp.einsum(
        "ixky,ixkz->kyz", parent_cols, second_cols, preferred_element_type=jnp.float32
    )
    diag_sum, cross_sum = lax.psum((diag_part, cross_part), "row")
    first_diag = diag_one.reshape(first_count, block, block) - diag_sum
    parent_diag = jnp.take(first_diag.astype(jnp.bfloat16), local_parent, axis=0)
    coupling = parent_block.reshape(second_count, block, block)
    parent_inv = (
        -(
            jnp.einsum("kyx,kxz->kyz", parent_diag, coupling, preferred_element_type=jnp.float32)
            + cross_sum
        )
    ).astype(jnp.bfloat16)
    second_total = add_rows(
        second_empty, lax.all_gather(second_factor, "row", axis=1, tiled=True), jnp.int32(0)
    )
    side = jnp.einsum("ixky,kyz->ixkz", parent_cols, coupling, preferred_element_type=jnp.float32)
    second_inv = (-(second_total.reshape(second_shape) + side) * second_keep).astype(jnp.bfloat16)
    child_part = jnp.einsum(
        "ixky,ixkz->kyz", second_cols, second_inv, preferred_element_type=jnp.float32
    )
    child_sum = lax.psum(child_part.astype(jnp.bfloat16), "row").astype(jnp.float32)
    parent_terms = jnp.einsum(
        "kxy,kxz->kyz", coupling, parent_inv, preferred_element_type=jnp.float32
    )
    second_diag = diag_two.reshape(second_count, block, block) - (child_sum + parent_terms)
    return (
        first_inv.reshape(factor_one.shape),
        first_diag.reshape(diag_one.shape),
        second_inv.reshape(factor_two.shape),
        parent_inv.reshape(parent_block.shape),
        second_diag.reshape(diag_two.shape),
    )


def solution(mesh):
    placed = (
        P(None, "row", None, None, "col", None),
        P(None, "row", None, None, "col", None),
        P(None, "row", None, None, "col", None),
        P(None, "col", None, None),
        P(None, "col", None, None),
        P(None, "col", None, None),
        P(None, "row", None, "col"),
        P(None, "row", None, "col"),
        P(None, "col"),
    )
    return jax.shard_map(
        body,
        mesh=mesh,
        in_specs=placed,
        out_specs=(
            P(None, "row", None, None, "col", None),
            P(None, "col", None, None),
            P(None, "row", None, None, "col", None),
            P(None, "col", None, None),
            P(None, "col", None, None),
        ),
        check_vma=False,
    )
```

profile of v0, /device:TPU:40, one launch (start us, length us, event | category | flops | bytes accessed | tf_op | source)
XLA Modules:
  0.0 917.3 jit_solution(8874706373367763510)
XLA Ops:
  7.2 0.0 copy-start
  7.2 0.0 all-gather.4.cloned.1.call-start
  7.2 0.7 convert_bitcast_fusion
  8.0 1.7 copy_multiply_fusion
  9.7 0.0 all-gather.4.cloned.1.call-update
  9.7 0.0 all-gather.6.cloned.1.call-start
  9.8 1.8 copy.41
  11.6 0.0 all-gather.6.cloned.1.call-update
  11.6 0.0 all-gather.8.cloned.1.call-start
  12.3 1.6 bitcast_multiply_fusion
  13.9 0.0 all-gather.8.cloned.1.call-update
  13.9 0.0 all-reduce.6.cloned.1.call-start
  14.6 0.6 dynamic-slice.9
  15.2 138.5 %all-gather.4.cloned.1.call-done = bf16[1,32,256,2,1,256]{5,2,4,3,0,1:T(8,128)(2,1)} async-done(((bf16[1,1,256,2,1,256]{5,2,4,3,0,1:T(8,128)(2,1)}), bf16[1,32,256,2,1,256]{5,2,4,3,0,1:T(8,128)(2,1)}) %all-gather.4.cloned.1.call-update) | async-done | bytes 8388624 | tf_op jit(solution)/shard_map/all_gather | solution.py:44
  153.7 14.6 %copy.40 = bf16[1,32,256,2,1,256]{2,1,5,3,4,0:T(8,128)(2,1)} copy(bf16[1,32,256,2,1,256]{5,2,4,3,0,1:T(8,128)(2,1)} %all-gather.4.cloned.1.call-done) | data formatting | bytes 16777216 | tf_op jit(solution)/shard_map/all_gather | solution.py:44
  168.4 16.5 %copy.53 = bf16[64,8,32,256]{3,1,2,0:T(8,128)(2,1)} copy(bf16[64,8,32,256]{3,2,1,0:T(8,128)(2,1)} %bitcast.112) | data formatting | bytes 16777216
  184.8 12.1 %all-gather.6.cloned.1.call-done = bf16[1,1,256,2,16,256]{2,5,4,3,1,0:T(8,128)(2,1)} async-done(((bf16[1,1,256,2,1,256]{2,5,4,3,1,0:T(8,128)(2,1)}), bf16[1,1,256,2,16,256]{2,5,4,3,1,0:T(8,128)(2,1)}) %all-gather.6.cloned.1.call-update) | async-done | bytes 4194320 | tf_op jit(solution)/shard_map/all_gather | solution.py:39
  196.9 0.0 copy-start.2
  196.9 0.0 copy-start.1
  196.9 7.2 convolution_negate_fusion
  204.1 0.2 copy.43
  204.3 0.0 copy-done.2
  204.3 1.5 convolution_bitcast_fusion.1
  205.8 0.0 copy-done.1
  205.8 1.1 fusion.11
  206.9 0.0 all-reduce.6.cloned.1.call-update
  207.0 0.0 all-reduce.4.cloned.1.call-start
  207.0 94.3 %all-gather.8.cloned.1.call-done = bf16[1,32,256,1,1,256]{5,2,4,3,0,1:T(8,128)(2,1)} async-done(((bf16[1,1,256,1,1,256]{5,2,4,3,0,1:T(8,128)(2,1)}), bf16[1,32,256,1,1,256]{5,2,4,3,0,1:T(8,128)(2,1)}) %all-gather.8.cloned.1.call-update) | async-done | bytes 4194320 | tf_op jit(solution)/shard_map/all_gather | solution.py:72
  301.3 4.8 convolution_bitcast_fusion.4
  306.1 0.0 copy-start.6
  306.1 0.2 copy.42
  306.4 0.0 copy-done
  306.4 0.9 fusion.9
  307.2 0.8 copy.49
  308.0 0.9 fusion.10
  308.9 0.9 multiply_convert_fusion.1
  309.8 0.0 all-reduce.4.cloned.1.call-update
  309.9 309.2 %all-reduce.6.cloned.1.call-done = (f32[2,256,256]{2,1,0:T(8,128)}, f32[1,256,256]{2,1,0:T(8,128)}) async-done(((f32[2,256,256]{2,1,0:T(8,128)}, f32[1,256,256]{2,1,0:T(8,128)}), (f32[2,256,256]{2,1,0:T(8,128)}, f32[1,256,256]{2,1,0:T(8,128)})) %all-reduce.6.cloned.1.call-update) | async-done | bytes 786448 | tf_op jit(solution)/shard_map/psum | solution.py:61
  619.1 0.0 copy-done.4
  619.1 1.1 bitcast_subtract_fusion
  620.2 0.0 copy-start.3
  620.2 1.3 fusion.8
  621.5 0.0 copy-start.5
  621.6 287.4 %all-reduce.4.cloned.1.call-done = bf16[1,256,256]{2,1,0:T(8,128)(2,1)} async-done(((bf16[1,256,256]{2,1,0:T(8,128)(2,1)}), bf16[1,256,256]{2,1,0:T(8,128)(2,1)}) %all-reduce.4.cloned.1.call-update) | async-done | bytes 131088 | tf_op jit(solution)/shard_map/psum | solution.py:79
  909.0 0.0 copy-done.6
  909.0 1.8 fusion.7
  910.8 0.0 copy-done.3
  910.8 0.0 copy-done.5
  (1 shorter events, 0.0 us)
Async XLA Ops:
  7.2 299.2 %copy-start = (bf16[1,1,256,256]{3,2,1,0:T(8,128)(2,1)S(1)}, bf16[1,1,256,256]{3,2,1,0:T(8,128)(2,1)}, u32[]{:S(2)}) copy-start(bf16[1,1,256,256]{3,2,1,0:T(8,128)(2,1)} %param.12) | copy-start | bytes 393220
  7.2 146.6 %all-gather.4.cloned.1.call-start = ((), (), s32[]{:S(2)}) async-start(), calls=%async_computation | async-start | bytes 8650752 | tf_op jit(solution)/shard_map/all_gather | solution.py:44
  9.7 187.2 %all-gather.6.cloned.1.call-start = ((), (), s32[]{:S(2)}) async-start(), calls=%async_computation.1 | async-start | bytes 4456448 | tf_op jit(solution)/shard_map/all_gather | solution.py:39
  11.6 289.7 %all-gather.8.cloned.1.call-start = ((), (), s32[]{:S(2)}) async-start(), calls=%async_computation.2 | async-start | bytes 4325376 | tf_op jit(solution)/shard_map/all_gather | solution.py:72
  13.9 605.2 %all-reduce.6.cloned.1.call-start = ((), (), s32[]{:S(2)}) async-start(), calls=%async_computation.4 | async-start | bytes 1572864 | tf_op jit(solution)/shard_map/psum | solution.py:61
  196.9 7.4 copy-start.2
  196.9 8.9 copy-start.1
  207.0 702.0 %all-reduce.4.cloned.1.call-start = ((), (), s32[]{:S(2)}) async-start(), calls=%async_computation.3 | async-start | bytes 262144 | tf_op jit(solution)/shard_map/psum | solution.py:79
  301.3 317.8 %copy-start.4 = (f32[2,1,256,256]{3,2,1,0:T(8,128)S(1)}, f32[2,1,256,256]{3,2,1,0:T(8,128)}, u32[]{:S(2)}) copy-start(f32[2,1,256,256]{3,2,1,0:T(8,128)} %param.13) | copy-start | bytes 1572868
  306.1 602.9 %copy-start.6 = (f32[1,1,256,256]{3,2,1,0:T(8,128)S(1)}, f32[1,1,256,256]{3,2,1,0:T(8,128)}, u32[]{:S(2)}) copy-start(f32[1,1,256,256]{3,2,1,0:T(8,128)} %param.14) | copy-start | bytes 786436
  620.2 290.6 %copy-start.3 = (f32[2,256,256]{2,1,0:T(8,128)}, f32[2,256,256]{2,1,0:T(8,128)S(1)}, u32[]{:S(2)}) copy-start(f32[2,256,256]{2,1,0:T(8,128)S(1)} %bitcast_subtract_fusion) | copy-start | bytes 1572868
  621.5 289.3 %copy-start.5 = (bf16[1,256,256]{2,1,0:T(8,128)(2,1)}, bf16[1,256,256]{2,1,0:T(8,128)(2,1)S(1)}, u32[]{:S(2)}) copy-start(bf16[1,256,256]{2,1,0:T(8,128)(2,1)S(1)} %fusion.8) | copy-start | bytes 393220
Sparse Core Ops, SparseCore 0:
  11.8 141.9 all-gather.3
  156.4 40.4 all-gather.5
  200.7 100.6 all-gather.7
  304.7 314.3 all-reduce.5
  622.7 286.2 all-reduce.3
where the time goes:
time: 918 us; the launch traced here: 917 us
  waiting for transfers between devices  842 us (92%)
  local copies, waits for them, and re-layouts  34.7 us (4%)
  matrix products  19.5 us (2%)
  between operations  15.2 us (2%)
    psum x1, waiting for transfers between devices, body(): diag_sum, cross_sum = lax.psum((diag_part, cross_part), 'row')  309 us
    psum x1, waiting for transfers between devices, body(): lax.psum(child_part.astype(jnp.bfloat16), 'row').astype(jnp.float32)  287 us
    all_gather x1, waiting for transfers between devices, body(): lax.all_gather(first_factor, 'row', axis=1, tiled=True)  139 us
    all_gather x1, waiting for transfers between devices, body(): lax.all_gather(second_factor, 'row', axis=1, tiled=True)  94.3 us
    unnamed x17, local copies, waits for them, and re-layouts  19.1 us
  transfers between devices with their start and end apart: 5, of which 5 were waited for; matrix products, arithmetic and copies ran while one was open for 6% of the time, Pallas kernels for 0%

commit v1 on v0

--- a/solution.py
+++ b/solution.py
@@ -41,7 +41,11 @@
     )
     add_rows = rows_step(whole_anc, anc_rows, block)
     first_total = add_rows(
-        first_empty, lax.all_gather(first_factor, "row", axis=1, tiled=True), jnp.int32(0)
+        first_empty,
+        jnp.concatenate(
+            lax.all_to_all(jnp.stack([first_factor] * lax.axis_size("row")), "row", 0, 0), axis=1
+        ),
+        jnp.int32(0),
     )
     first_shape = (anc_rows, block, first_count, block)
     second_shape = (anc_rows, block, second_count, block)

time: 918 us -> 974 us (1.061)
  waiting for transfers between devices: 842 us -> 883 us
  starting transfers between devices: 0.21 us -> 16.2 us
    all_to_all x0 -> x1, waiting for transfers between devices: none -> 254 us  [body(): lax.all_to_all(jnp.stack([first_factor] * lax.axis_size('row')), 'row', 0...]
    all_gather x1 -> x0, waiting for transfers between devices: 139 us -> none  [body(): lax.all_gather(first_factor, 'row', axis=1, tiled=True)]
    all_gather x1, waiting for transfers between devices: 94.3 us -> 32.2 us  [body(): lax.all_gather(second_factor, 'row', axis=1, tiled=True)]
    all_to_all x0 -> x1, starting transfers between devices: none -> 16 us  [body(): lax.all_to_all(jnp.stack([first_factor] * lax.axis_size('row')), 'row', 0...]
    all_gather x1 -> x0, local copies, waits for them, and re-layouts: 14.6 us -> none  [body(): lax.all_gather(first_factor, 'row', axis=1, tiled=True)]
    all_gather x1, waiting for transfers between devices: 12.1 us -> 0.01 us  [body(): lax.all_gather(anc_inverse, 'col', axis=4, tiled=True)]
    all_to_all x0 -> x1, local copies, waits for them, and re-layouts: none -> 11.4 us  [body(): lax.all_to_all(jnp.stack([first_factor] * lax.axis_size('row')), 'row', 0...]
  transfers between devices with their start and end apart: 5 -> 5, of which waited for: 5 -> 4; matrix products, arithmetic and copies ran while one was open for 6% -> 5% of each run, Pallas kernels for 0% -> 0%
where the time goes in v1:
time: 974 us
  waiting for transfers between devices  883 us (91%)
  local copies, waits for them, and re-layouts  35.2 us (4%)
  matrix products  19.3 us (2%)
  starting transfers between devices  16.2 us (2%)
  between operations  15.2 us (2%)
    psum x1, waiting for transfers between devices, body(): diag_sum, cross_sum = lax.psum((diag_part, cross_part), 'row')  310 us
    psum x1, waiting for transfers between devices, body(): lax.psum(child_part.astype(jnp.bfloat16), 'row').astype(jnp.float32)  287 us
    all_to_all x1, waiting for transfers between devices, body(): lax.all_to_all(jnp.stack([first_factor] * lax.axis_size('row')), 'row', 0...  254 us
    all_gather x1, waiting for transfers between devices, body(): lax.all_gather(second_factor, 'row', axis=1, tiled=True)  32.2 us
  transfers between devices with their start and end apart: 5, of which 4 were waited for; matrix products, arithmetic and copies ran while one was open for 5% of the time, Pallas kernels for 0%

profile of v1, /device:TPU:40, one launch (start us, length us, event | category | flops | bytes accessed | tf_op | source)
XLA Modules:
  0.0 973.9 jit_solution(10576325178377848750)
XLA Ops:
  7.2 0.0 copy-start
  7.2 0.7 convert_bitcast_fusion
  7.9 1.2 multiply_bitcast_fusion
  9.2 0.2 copy.30
  9.3 4.3 stack.2
  13.6 0.0 copy-start.6
  13.6 16.0 %all-to-all-start = ((bf16[32,1,1,256,2,1,256]{3,6,4,5,2,1,0:T(8,128)(2,1)}), bf16[32,1,1,256,2,1,256]{3,6,4,5,2,1,0:T(8,128)(2,1)}, u32[]{:S(2)}, u32[]{:S(2)}) async-start(bf16[32,1,1,256,2,1,256]{3,6,4,5,2,1,0:T(8,128)(2,1)} %stack.2), calls=%async_computation | async-start | bytes 16777216 | tf_op jit(solution)/shard_map/all_to_all | solution.py:46
  29.6 0.0 all-gather.3.cloned.1.call-start
  29.7 0.0 copy-done.6
  29.7 0.9 copy.32
  30.6 0.0 all-gather.3.cloned.1.call-update
  30.6 0.0 all-gather.5.cloned.1.call-start
  31.3 0.0 copy-done.7
  31.3 0.7 bitcast_multiply_fusion
  32.0 0.0 all-gather.5.cloned.1.call-update
  32.0 0.0 all-reduce.6.cloned.1.call-start
  32.7 0.6 dynamic-slice.9
  33.3 254.5 %all-to-all-done = bf16[32,1,1,256,2,1,256]{3,6,4,5,2,1,0:T(8,128)(2,1)} async-done(((bf16[32,1,1,256,2,1,256]{3,6,4,5,2,1,0:T(8,128)(2,1)}), bf16[32,1,1,256,2,1,256]{3,6,4,5,2,1,0:T(8,128)(2,1)}, u32[]{:S(2)}, u32[]{:S(2)}) %all-to-all-start) | async-done | bytes 8388640 | tf_op jit(solution)/shard_map/all_to_all | solution.py:46
  287.8 11.4 %copy.31 = bf16[32,1,1,256,2,1,256]{3,0,6,4,5,2,1:T(8,128)(2,1)} copy(bf16[32,1,1,256,2,1,256]{3,6,4,5,2,1,0:T(8,128)(2,1)} %all-to-all-done) | data formatting | bytes 16777216 | tf_op jit(solution)/shard_map/all_to_all | solution.py:46
  299.2 16.6 %copy.43 = bf16[64,8,32,256]{3,1,2,0:T(8,128)(2,1)} copy(bf16[64,8,32,256]{3,2,1,0:T(8,128)(2,1)} %bitcast.112) | data formatting | bytes 16777216
  315.8 7.0 convolution_negate_fusion
  322.8 0.2 copy.34
  323.1 0.0 copy-done.1
  323.1 1.5 convolution_bitcast_fusion.1
  324.6 1.1 fusion.11
  325.7 0.0 all-reduce.6.cloned.1.call-update
  325.7 0.0 all-reduce.4.cloned.1.call-start
  325.8 32.2 %all-gather.5.cloned.1.call-done = bf16[1,32,256,1,1,256]{5,2,4,3,0,1:T(8,128)(2,1)} async-done(((bf16[1,1,256,1,1,256]{5,2,4,3,0,1:T(8,128)(2,1)}), bf16[1,32,256,1,1,256]{5,2,4,3,0,1:T(8,128)(2,1)}) %all-gather.5.cloned.1.call-update) | async-done | bytes 4194320 | tf_op jit(solution)/shard_map/all_gather | solution.py:76
  357.9 4.8 convolution_bitcast_fusion.4
  362.7 0.0 copy-start.5
  362.7 0.2 copy.33
  363.0 0.0 copy-done
  363.0 0.9 fusion.9
  363.9 0.8 copy.40
  364.6 0.9 fusion.10
  365.5 0.9 multiply_convert_fusion.1
  366.4 0.0 all-reduce.4.cloned.1.call-update
  366.5 309.7 %all-reduce.6.cloned.1.call-done = (f32[2,256,256]{2,1,0:T(8,128)}, f32[1,256,256]{2,1,0:T(8,128)}) async-done(((f32[2,256,256]{2,1,0:T(8,128)}, f32[1,256,256]{2,1,0:T(8,128)}), (f32[2,256,256]{2,1,0:T(8,128)}, f32[1,256,256]{2,1,0:T(8,128)})) %all-reduce.6.cloned.1.call-update) | async-done | bytes 786448 | tf_op jit(solution)/shard_map/psum | solution.py:65
  676.1 0.0 copy-done.3
  676.2 1.1 bitcast_subtract_fusion
  677.3 0.0 copy-start.2
  677.3 1.3 fusion.8
  678.6 0.0 copy-start.4
  678.6 286.8 %all-reduce.4.cloned.1.call-done = bf16[1,256,256]{2,1,0:T(8,128)(2,1)} async-done(((bf16[1,256,256]{2,1,0:T(8,128)(2,1)}), bf16[1,256,256]{2,1,0:T(8,128)(2,1)}) %all-reduce.4.cloned.1.call-update) | async-done | bytes 131088 | tf_op jit(solution)/shard_map/psum | solution.py:83
  965.5 0.0 copy-done.5
  965.5 1.8 fusion.7
  967.3 0.0 copy-done.2
  967.3 0.0 copy-done.4
  (4 shorter events, 0.0 us)
Async XLA Ops:
  7.2 355.8 %copy-start = (bf16[1,1,256,256]{3,2,1,0:T(8,128)(2,1)S(1)}, bf16[1,1,256,256]{3,2,1,0:T(8,128)(2,1)}, u32[]{:S(2)}) copy-start(bf16[1,1,256,256]{3,2,1,0:T(8,128)(2,1)} %param.12) | copy-start | bytes 393220
  13.6 16.1 %copy-start.6 = (bf16[1,1,256,2,1,256]{5,3,4,2,1,0:T(2,128)(2,1)S(1)}, bf16[1,1,256,2,1,256]{5,3,4,2,1,0:T(2,128)(2,1)}, u32[]{:S(2)}) copy-start(bf16[1,1,256,2,1,256]{5,3,4,2,1,0:T(2,128)(2,1)} %param.9) | copy-start | bytes 786436
  13.6 17.7 %copy-start.7 = (bf16[1,1,256,1,1,256]{5,2,4,3,1,0:T(8,128)(2,1)S(1)}, bf16[1,1,256,1,1,256]{5,2,4,3,1,0:T(8,128)(2,1)}, u32[]{:S(2)}) copy-start(bf16[1,1,256,1,1,256]{5,2,4,3,1,0:T(8,128)(2,1)} %param.11) | copy-start | bytes 393220
  13.6 274.2 %all-to-all-start = ((bf16[32,1,1,256,2,1,256]{3,6,4,5,2,1,0:T(8,128)(2,1)}), bf16[32,1,1,256,2,1,256]{3,6,4,5,2,1,0:T(8,128)(2,1)}, u32[]{:S(2)}, u32[]{:S(2)}) async-start(bf16[32,1,1,256,2,1,256]{3,6,4,5,2,1,0:T(8,128)(2,1)} %stack.2), calls=%async_computation | async-start | bytes 16777216 | tf_op jit(solution)/shard_map/all_to_all | solution.py:46
  29.6 286.2 %all-gather.3.cloned.1.call-start = ((), (), s32[]{:S(2)}) async-start(), calls=%async_computation.1 | async-start | bytes 4456448 | tf_op jit(solution)/shard_map/all_gather | solution.py:39
  30.6 327.3 %all-gather.5.cloned.1.call-start = ((), (), s32[]{:S(2)}) async-start(), calls=%async_computation.2 | async-start | bytes 4325376 | tf_op jit(solution)/shard_map/all_gather | solution.py:76
  32.0 644.1 %all-reduce.6.cloned.1.call-start = ((), (), s32[]{:S(2)}) async-start(), calls=%async_computation.4 | async-start | bytes 1572864 | tf_op jit(solution)/shard_map/psum | solution.py:65
  315.8 7.2 copy-start.1
  325.7 639.7 %all-reduce.4.cloned.1.call-start = ((), (), s32[]{:S(2)}) async-start(), calls=%async_computation.3 | async-start | bytes 262144 | tf_op jit(solution)/shard_map/psum | solution.py:83
  357.9 318.2 %copy-start.3 = (f32[2,1,256,256]{3,2,1,0:T(8,128)S(1)}, f32[2,1,256,256]{3,2,1,0:T(8,128)}, u32[]{:S(2)}) copy-start(f32[2,1,256,256]{3,2,1,0:T(8,128)} %param.13) | copy-start | bytes 1572868
  362.7 602.8 %copy-start.5 = (f32[1,1,256,256]{3,2,1,0:T(8,128)S(1)}, f32[1,1,256,256]{3,2,1,0:T(8,128)}, u32[]{:S(2)}) copy-start(f32[1,1,256,256]{3,2,1,0:T(8,128)} %param.14) | copy-start | bytes 786436
  677.3 290.1 %copy-start.2 = (f32[2,256,256]{2,1,0:T(8,128)}, f32[2,256,256]{2,1,0:T(8,128)S(1)}, u32[]{:S(2)}) copy-start(f32[2,256,256]{2,1,0:T(8,128)S(1)} %bitcast_subtract_fusion) | copy-start | bytes 1572868
  678.6 288.7 %copy-start.4 = (bf16[1,256,256]{2,1,0:T(8,128)(2,1)}, bf16[1,256,256]{2,1,0:T(8,128)(2,1)S(1)}, u32[]{:S(2)}) copy-start(bf16[1,256,256]{2,1,0:T(8,128)(2,1)S(1)} %fusion.8) | copy-start | bytes 393220
Sparse Core Ops, SparseCore 0:
  33.1 113.5 all-gather.2
  150.5 207.3 all-gather.4
  361.5 314.6 all-reduce.5
  679.2 286.2 all-reduce.3
